TPU v7x, 512 devices: a whole 4x4x16 slice. The times are simulated.
512 devices in a mesh: row: 32 (over x, z_lo), col: 16 (over z_hi, y, core).
Axes of the slice: x: 4, y: 4, z: 16 (z_hi: 2, z_lo: 8; z = z_hi * 8 + z_lo), core: 2. Of those that a mesh axis runs over, the one named last changes fastest.
Arguments:
- amplitudes: float32 [3072, 4, 2048], P(('row', 'col')), may hold values from -6 to 6
- integrals: float32 [8192, 4, 2048], P('row', None, 'col'), may hold values from -0.0625 to 0.0625
Outputs:
- ladder: float32 [3072, 8192], P('col', 'row')
All inputs are finite; a program needn't handle non-finite values.
Results may differ from a plain program's by a relative error of at most 0.0001.
Values sent between devices are 32-bit elements; how exact they have to be, the bound alone decides.
No kernel may reach another device: no remote copies, remote signals or barrier semaphores. Data moves between devices by JAX's collectives and lax.ppermute only.
A program may use at most 64 MiB of HBM per device.

v0:
```python
import jax
import jax.numpy as jnp
from jax import lax
from jax.sharding import PartitionSpec as P

PANELS = 4


def contract(rows, weights):
    return lax.dot_general(
        rows,
        weights,
        (((1,), (1,)), ((), ())),
        precision=lax.Precision.HIGHEST,
        preferred_element_type=jnp.float32,
    )


def per_device(amplitudes, integrals):
    n_row = lax.axis_size("row")
    n_col = lax.axis_size("col")
    local_rows = amplitudes.shape[0]
    width = integrals.shape[2]
    all_rows = local_rows * n_row * n_col
    total = jnp.zeros((all_rows, integrals.shape[0]), jnp.float32)
    for panel in range(PANELS):
        piece = amplitudes[:, panel, :]
        weights = integrals[:, panel, :]
        spread = lax.all_gather(piece, "row", axis=0, tiled=True)
        mixed = lax.all_to_all(spread, "col", split_axis=1, concat_axis=0, tiled=True)
        ordered = (
            mixed.reshape(n_col, n_row, local_rows, width)
            .transpose(1, 0, 2, 3)
            .reshape(all_rows, width)
        )
        total = total + contract(ordered, weights)
    return lax.psum_scatter(total, "col", scatter_dimension=0, tiled=True)


def solution(mesh):
    in_specs = (P(("row", "col"), None, None), P("row", None, "col"))
    out_specs = P("col", "row")
    return jax.shard_map(
        per_device, mesh=mesh, in_specs=in_specs, out_specs=out_specs, check_vma=False
    )
```

profile of v0, /device:TPU:2, one launch (start us, length us, event | category | flops | bytes accessed | tf_op | source)
XLA Modules:
  0.0 1254.1 jit_solution(16290584040939222164)
XLA Ops:
  6.5 0.0 all-gather.9.cloned.1.call-start
  6.5 2.1 fusion.1
  8.6 0.0 all-gather.9.cloned.1.call-update
  8.6 212.2 %all-gather.9.cloned.1.call-done = f32[192,1,2048]{2,1,0:T(1,128)} async-done(((f32[6,1,2048]{2,1,0:T(1,128)}), f32[192,1,2048]{2,1,0:T(1,128)}) %all-gather.9.cloned.1.call-update) | async-done | bytes 1572880 | tf_op jit(solution)/shard_map/all_gather | solution.py:29
  220.8 3.1 copy.7
  223.8 14.5 %all-to-all-start = ((f32[192,16,128]{2,0,1:T(8,128)}), f32[192,16,128]{2,0,1:T(8,128)S(1)}, u32[]{:S(2)}, u32[]{:S(2)}) async-start(f32[192,16,128]{2,0,1:T(8,128)} %copy.7), calls=%async_computation | async-start | bytes 3145728 | tf_op jit(solution)/shard_map/all_to_all | solution.py:30
  238.3 0.0 all-gather.11.cloned.1.call-start
  238.4 0.7 all-gather.11.cloned.1.call-update
  239.1 246.0 %all-gather.11.cloned.1.call-done = f32[192,1,2048]{2,1,0:T(1,128)} async-done(((f32[6,1,2048]{2,1,0:T(1,128)}), f32[192,1,2048]{2,1,0:T(1,128)}) %all-gather.11.cloned.1.call-update) | async-done | bytes 1572880 | tf_op jit(solution)/shard_map/all_gather | solution.py:29
  485.1 3.1 copy.10
  488.2 0.0 all-to-all-done
  488.2 7.6 all-to-all-start.1
  495.8 0.0 all-gather.13.cloned.1.call-start
  495.8 0.7 all-gather.13.cloned.1.call-update
  496.5 246.0 %all-gather.13.cloned.1.call-done = f32[192,1,2048]{2,1,0:T(1,128)} async-done(((f32[6,1,2048]{2,1,0:T(1,128)}), f32[192,1,2048]{2,1,0:T(1,128)}) %all-gather.13.cloned.1.call-update) | async-done | bytes 1572880 | tf_op jit(solution)/shard_map/all_gather | solution.py:29
  742.6 3.1 copy.13
  745.7 0.0 all-to-all-done.1
  745.7 1.2 copy-done
  746.9 8.1 all-to-all-start.2
  755.0 0.0 all-gather.15.cloned.1.call-start
  755.0 0.5 all-gather.15.cloned.1.call-update
  755.6 247.4 %all-gather.15.cloned.1.call-done = f32[192,1,2048]{2,1,0:T(1,128)} async-done(((f32[6,1,2048]{2,1,0:T(1,128)}), f32[192,1,2048]{2,1,0:T(1,128)}) %all-gather.15.cloned.1.call-update) | async-done | bytes 1572880 | tf_op jit(solution)/shard_map/all_gather | solution.py:29
  1002.9 3.1 copy.16
  1006.0 0.0 all-to-all-done.2
  1006.0 8.0 all-to-all-start.3
  1014.0 0.2 reduce-scatter.2.cloned.1.call-start
  1014.3 0.4 fusion
  1014.6 0.9 copy.8
  1015.6 0.6 copy.9
  1016.2 1.4 reshape.41
  1017.5 2.3 copy.11
  1019.9 0.6 copy.12
  1020.5 1.4 reshape.43
  1021.9 2.3 copy.14
  1024.2 0.6 copy.15
  1024.8 1.4 reshape.45
  1026.2 61.0 %all-to-all-done.3 = f32[192,16,128]{2,0,1:T(8,128)} async-done(((f32[192,16,128]{2,0,1:T(8,128)}), f32[192,16,128]{2,0,1:T(8,128)}, u32[]{:S(2)}, u32[]{:S(2)}) %all-to-all-start.3) | async-done | bytes 1572896 | tf_op jit(solution)/shard_map/all_to_all | solution.py:30
  1087.2 2.3 copy.17
  1089.5 0.6 copy.18
  1090.1 1.3 reshape.47
  1091.5 4.2 fusion.2
  1095.7 0.0 copy-done.1
  1095.7 0.0 copy-start.2
  1095.7 2.9 convolution_add_fusion.2
  1098.6 2.7 convolution_add_fusion.1
  1101.4 4.3 convolution_add_fusion
  1105.7 0.0 reduce-scatter.2.cloned.1.call-update
  1105.7 141.9 %reduce-scatter.2.cloned.1.call-done = f32[192,256]{1,0:T(8,128)} async-done(((f32[3072,256]{1,0:T(8,128)}), f32[192,256]{1,0:T(8,128)}) %reduce-scatter.2.cloned.1.call-update) | async-done | bytes 196624 | tf_op jit(solution)/shard_map/reduce_scatter | solution.py:37
  (7 shorter events, 0.0 us)
Async XLA Ops:
  6.5 214.2 %all-gather.9.cloned.1.call-start = ((), (), s32[]{:S(2)}) async-start(), calls=%async_computation.6 | async-start | bytes 1622016 | tf_op jit(solution)/shard_map/all_gather | solution.py:29
  223.8 264.3 %all-to-all-start = ((f32[192,16,128]{2,0,1:T(8,128)}), f32[192,16,128]{2,0,1:T(8,128)S(1)}, u32[]{:S(2)}, u32[]{:S(2)}) async-start(f32[192,16,128]{2,0,1:T(8,128)} %copy.7), calls=%async_computation | async-start | bytes 3145728 | tf_op jit(solution)/shard_map/all_to_all | solution.py:30
  238.3 246.8 %all-gather.11.cloned.1.call-start = ((), (), s32[]{:S(2)}) async-start(), calls=%async_computation.7 | async-start | bytes 1622016 | tf_op jit(solution)/shard_map/all_gather | solution.py:29
  488.2 257.5 %all-to-all-start.1 = ((f32[192,16,128]{2,0,1:T(8,128)}), f32[192,16,128]{2,0,1:T(8,128)S(1)}, u32[]{:S(2)}, u32[]{:S(2)}) async-start(f32[192,16,128]{2,0,1:T(8,128)} %copy.10), calls=%async_computation.1 | async-start | bytes 3145728 | tf_op jit(solution)/shard_map/all_to_all | solution.py:30
  495.8 246.8 %all-gather.13.cloned.1.call-start = ((), (), s32[]{:S(2)}) async-start(), calls=%async_computation.8 | async-start | bytes 1622016 | tf_op jit(solution)/shard_map/all_gather | solution.py:29
  745.7 1.2 copy-start
  746.9 259.1 %all-to-all-start.2 = ((f32[192,16,128]{2,0,1:T(8,128)}), f32[192,16,128]{2,0,1:T(8,128)}, u32[]{:S(2)}, u32[]{:S(2)}) async-start(f32[192,16,128]{2,0,1:T(8,128)} %copy.13), calls=%async_computation.2 | async-start | bytes 3145728 | tf_op jit(solution)/shard_map/all_to_all | solution.py:30
  755.0 247.9 %all-gather.15.cloned.1.call-start = ((), (), s32[]{:S(2)}) async-start(), calls=%async_computation.9 | async-start | bytes 1622016 | tf_op jit(solution)/shard_map/all_gather | solution.py:29
  1006.0 8.3 copy-start.4
  1006.0 81.2 %all-to-all-start.3 = ((f32[192,16,128]{2,0,1:T(8,128)}), f32[192,16,128]{2,0,1:T(8,128)}, u32[]{:S(2)}, u32[]{:S(2)}) async-start(f32[192,16,128]{2,0,1:T(8,128)} %copy.16), calls=%async_computation.3 | async-start | bytes 3145728 | tf_op jit(solution)/shard_map/all_to_all | solution.py:30
  1014.0 233.6 %reduce-scatter.2.cloned.1.call-start = ((), (), s32[]{:S(2)}) async-start(), calls=%async_computation.5 | async-start | bytes 3342336 | tf_op jit(solution)/shard_map/reduce_scatter | solution.py:37
  1091.4 4.2 copy-start.1
  1095.7 3.0 copy-start.2
  1098.6 2.7 copy-start.3
Sparse Core Ops, SparseCore 0:
  9.4 211.3 all-gather.8
  241.2 243.8 all-gather.10
  498.7 243.8 all-gather.12
  757.6 245.3 all-gather.14
  1105.8 141.7 reduce-scatter.1
where the time goes:
time: 1250 us
  waiting for transfers between devices  1160 us (93%)
  starting transfers between devices  38.5 us (3%)
  local copies, waits for them, and re-layouts  31.7 us (3%)
  matrix products  14.1 us (1%)
  between operations  13.3 us (1%)
    all_gather x4, waiting for transfers between devices, per_device(): spread = lax.all_gather(piece, 'row', axis=0, tiled=True)  952 us
    reduce_scatter x1, waiting for transfers between devices, per_device(): return lax.psum_scatter(total, 'col', scatter_dimension=0, tiled=True)  142 us
    all_to_all x4, waiting for transfers between devices, per_device(): lax.all_to_all(spread, 'col', split_axis=1, concat_axis=0, tiled=True)  61 us
    all_to_all x4, starting transfers between devices, per_device(): lax.all_to_all(spread, 'col', split_axis=1, concat_axis=0, tiled=True)  38.2 us
  transfers between devices with their start and end apart: 9, of which 6 were waited for; matrix products, arithmetic and copies ran while one was open for 2% of the time, Pallas kernels for 0%

commit v1 on v0

--- a/solution.py
+++ b/solution.py
@@ -26,7 +26,10 @@
     for panel in range(PANELS):
         piece = amplitudes[:, panel, :]
         weights = integrals[:, panel, :]
-        spread = lax.all_gather(piece, "row", axis=0, tiled=True)
+        size = lax.axis_size("row")
+        tiles = jnp.stack([piece for _ in range(size)])
+        tiles = lax.all_to_all(tiles, "row", split_axis=0, concat_axis=0)
+        spread = jnp.concatenate(tiles, axis=0)
         mixed = lax.all_to_all(spread, "col", split_axis=1, concat_axis=0, tiled=True)
         ordered = (
             mixed.reshape(n_col, n_row, local_rows, width)

time: 1250 us -> 926 us (0.74)
  waiting for transfers between devices: 1160 us -> 771 us
  starting transfers between devices: 38.5 us -> 83.8 us
    all_gather x4 -> x0, waiting for transfers between devices: 952 us -> none  [per_device(): spread = lax.all_gather(piece, 'row', axis=0, tiled=True)]
    all_to_all x0 -> x4, waiting for transfers between devices: none -> 357 us  [per_device(): tiles = lax.all_to_all(tiles, 'row', split_axis=0, concat_axis=0)]
    all_to_all x4, waiting for transfers between devices: 61 us -> 192 us  [per_device(): lax.all_to_all(spread, 'col', split_axis=1, concat_axis=0, tiled=True)]
    reduce_scatter x1, waiting for transfers between devices: 142 us -> 222 us  [per_device(): return lax.psum_scatter(total, 'col', scatter_dimension=0, tiled=True)]
    all_to_all x0 -> x4, starting transfers between devices: none -> 50.2 us  [per_device(): tiles = lax.all_to_all(tiles, 'row', split_axis=0, concat_axis=0)]
    all_to_all x8 -> x12, local copies, waits for them, and re-layouts: 20.2 us -> 25.6 us  [per_device(): lax.all_to_all(spread, 'col', split_axis=1, concat_axis=0, tiled=True)]
  transfers between devices with their start and end apart: 9 -> 9, of which waited for: 6 -> 9; matrix products, arithmetic and copies ran while one was open for 2% -> 2% of each run, Pallas kernels for 0% -> 0%
where the time goes in v1:
time: 926 us; the launch traced here: 925 us
  waiting for transfers between devices  771 us (83%)
  starting transfers between devices  83.8 us (9%)
  local copies, waits for them, and re-layouts  42.9 us (5%)
  matrix products  14.2 us (2%)
  between operations  13.6 us (1%)
    all_to_all x4, waiting for transfers between devices, per_device(): tiles = lax.all_to_all(tiles, 'row', split_axis=0, concat_axis=0)  357 us
    reduce_scatter x1, waiting for transfers between devices, per_device(): return lax.psum_scatter(total, 'col', scatter_dimension=0, tiled=True)  222 us
    all_to_all x4, waiting for transfers between devices, per_device(): lax.all_to_all(spread, 'col', split_axis=1, concat_axis=0, tiled=True)  192 us
    all_to_all x4, starting transfers between devices, per_device(): tiles = lax.all_to_all(tiles, 'row', split_axis=0, concat_axis=0)  50.2 us
    all_to_all x4, starting transfers between devices, per_device(): lax.all_to_all(spread, 'col', split_axis=1, concat_axis=0, tiled=True)  33.4 us
    all_to_all x12, local copies, waits for them, and re-layouts, per_device(): lax.all_to_all(spread, 'col', split_axis=1, concat_axis=0, tiled=True)  25.6 us
  transfers between devices with their start and end apart: 9, of which 9 were waited for; matrix products, arithmetic and copies ran while one was open for 2% of the time, Pallas kernels for 0%

profile of v1, /device:TPU:2, one launch (start us, length us, event | category | flops | bytes accessed | tf_op | source)
XLA Modules:
  0.0 925.2 jit_solution(8790647642855032254)
XLA Ops:
  6.5 1.4 fusion.1
  8.0 1.6 stack.12
  9.6 15.7 %all-to-all-start = ((f32[32,6,2048]{2,1,0:T(8,128)}), f32[32,6,2048]{2,1,0:T(8,128)S(1)}, u32[]{:S(2)}, u32[]{:S(2)}) async-start(f32[32,6,2048]{2,1,0:T(8,128)} %stack.12), calls=%async_computation | async-start | bytes 4194304 | tf_op jit(solution)/shard_map/all_to_all | solution.py:31
  25.3 90.8 %all-to-all-done = f32[32,6,2048]{2,1,0:T(8,128)S(1)} async-done(((f32[32,6,2048]{2,1,0:T(8,128)}), f32[32,6,2048]{2,1,0:T(8,128)S(1)}, u32[]{:S(2)}, u32[]{:S(2)}) %all-to-all-start) | async-done | bytes 1572896 | tf_op jit(solution)/shard_map/all_to_all | solution.py:31
  116.1 1.6 stack.13
  117.6 11.5 %all-to-all-start.2 = ((f32[32,6,2048]{2,1,0:T(8,128)}), f32[32,6,2048]{2,1,0:T(8,128)}, u32[]{:S(2)}, u32[]{:S(2)}) async-start(f32[32,6,2048]{2,1,0:T(8,128)} %stack.13), calls=%async_computation.2 | async-start | bytes 4194304 | tf_op jit(solution)/shard_map/all_to_all | solution.py:31
  129.2 90.6 %all-to-all-done.2 = f32[32,6,2048]{2,1,0:T(8,128)} async-done(((f32[32,6,2048]{2,1,0:T(8,128)}), f32[32,6,2048]{2,1,0:T(8,128)}, u32[]{:S(2)}, u32[]{:S(2)}) %all-to-all-start.2) | async-done | bytes 1572896 | tf_op jit(solution)/shard_map/all_to_all | solution.py:31
  219.8 1.6 stack.14
  221.4 11.5 %all-to-all-start.4 = ((f32[32,6,2048]{2,1,0:T(8,128)}), f32[32,6,2048]{2,1,0:T(8,128)}, u32[]{:S(2)}, u32[]{:S(2)}) async-start(f32[32,6,2048]{2,1,0:T(8,128)} %stack.14), calls=%async_computation.4 | async-start | bytes 4194304 | tf_op jit(solution)/shard_map/all_to_all | solution.py:31
  232.9 90.1 %all-to-all-done.4 = f32[32,6,2048]{2,1,0:T(8,128)} async-done(((f32[32,6,2048]{2,1,0:T(8,128)}), f32[32,6,2048]{2,1,0:T(8,128)}, u32[]{:S(2)}, u32[]{:S(2)}) %all-to-all-start.4) | async-done | bytes 1572896 | tf_op jit(solution)/shard_map/all_to_all | solution.py:31
  323.0 1.6 stack.15
  324.6 11.6 %all-to-all-start.6 = ((f32[32,6,2048]{2,1,0:T(8,128)}), f32[32,6,2048]{2,1,0:T(8,128)}, u32[]{:S(2)}, u32[]{:S(2)}) async-start(f32[32,6,2048]{2,1,0:T(8,128)} %stack.15), calls=%async_computation.6 | async-start | bytes 4194304 | tf_op jit(solution)/shard_map/all_to_all | solution.py:31
  336.2 1.7 all_to_all.61
  337.9 3.1 copy.24
  341.0 85.4 %all-to-all-done.6 = f32[32,6,2048]{2,1,0:T(8,128)} async-done(((f32[32,6,2048]{2,1,0:T(8,128)}), f32[32,6,2048]{2,1,0:T(8,128)}, u32[]{:S(2)}, u32[]{:S(2)}) %all-to-all-start.6) | async-done | bytes 1572896 | tf_op jit(solution)/shard_map/all_to_all | solution.py:31
  426.4 10.3 %all-to-all-start.1 = ((f32[192,16,128]{2,0,1:T(8,128)}), f32[192,16,128]{2,0,1:T(8,128)S(1)}, u32[]{:S(2)}, u32[]{:S(2)}) async-start(f32[192,16,128]{2,0,1:T(8,128)} %copy.24), calls=%async_computation.1 | async-start | bytes 3145728 | tf_op jit(solution)/shard_map/all_to_all | solution.py:33
  436.7 1.9 all_to_all.65
  438.6 1.7 copy.28
  440.3 31.3 %all-to-all-done.1 = f32[192,16,128]{2,0,1:T(8,128)S(1)} async-done(((f32[192,16,128]{2,0,1:T(8,128)}), f32[192,16,128]{2,0,1:T(8,128)S(1)}, u32[]{:S(2)}, u32[]{:S(2)}) %all-to-all-start.1) | async-done | bytes 1572896 | tf_op jit(solution)/shard_map/all_to_all | solution.py:33
  471.6 3.7 all-to-all-start.3
  475.3 2.8 all_to_all.69
  478.1 3.1 copy.32
  481.2 52.6 %all-to-all-done.3 = f32[192,16,128]{2,0,1:T(8,128)S(1)} async-done(((f32[192,16,128]{2,0,1:T(8,128)}), f32[192,16,128]{2,0,1:T(8,128)S(1)}, u32[]{:S(2)}, u32[]{:S(2)}) %all-to-all-start.3) | async-done | bytes 1572896 | tf_op jit(solution)/shard_map/all_to_all | solution.py:33
  533.8 1.2 copy-done
  535.0 14.0 %all-to-all-start.5 = ((f32[192,16,128]{2,0,1:T(8,128)}), f32[192,16,128]{2,0,1:T(8,128)}, u32[]{:S(2)}, u32[]{:S(2)}) async-start(f32[192,16,128]{2,0,1:T(8,128)} %copy.32), calls=%async_computation.5 | async-start | bytes 3145728 | tf_op jit(solution)/shard_map/all_to_all | solution.py:33
  549.0 1.9 all_to_all.73
  550.9 1.6 copy.36
  552.5 58.3 %all-to-all-done.5 = f32[192,16,128]{2,0,1:T(8,128)} async-done(((f32[192,16,128]{2,0,1:T(8,128)}), f32[192,16,128]{2,0,1:T(8,128)}, u32[]{:S(2)}, u32[]{:S(2)}) %all-to-all-start.5) | async-done | bytes 1572896 | tf_op jit(solution)/shard_map/all_to_all | solution.py:33
  610.9 5.3 all-to-all-start.7
  616.4 0.4 fusion
  616.8 0.9 copy.25
  617.7 0.6 copy.26
  618.4 1.3 reshape.57
  619.7 2.3 copy.29
  622.0 0.6 copy.30
  622.6 1.4 reshape.59
  624.0 2.3 copy.33
  626.4 0.6 copy.34
  627.0 1.3 reshape.61
  628.3 50.0 %all-to-all-done.7 = f32[192,16,128]{2,0,1:T(8,128)} async-done(((f32[192,16,128]{2,0,1:T(8,128)}), f32[192,16,128]{2,0,1:T(8,128)}, u32[]{:S(2)}, u32[]{:S(2)}) %all-to-all-start.7) | async-done | bytes 1572896 | tf_op jit(solution)/shard_map/all_to_all | solution.py:33
  678.3 2.3 copy.37
  680.7 0.6 copy.38
  681.3 1.3 reshape.63
  682.6 4.2 fusion.2
  686.8 2.9 convolution_add_fusion.2
  689.8 2.7 convolution_add_fusion.1
  692.5 4.3 convolution_add_fusion
  696.9 221.5 %reduce-scatter.2.cloned.1.call-done = f32[192,256]{1,0:T(8,128)} async-done(((f32[3072,256]{1,0:T(8,128)}), f32[192,256]{1,0:T(8,128)}) %reduce-scatter.2.cloned.1.call-update) | async-done | bytes 196624 | tf_op jit(solution)/shard_map/reduce_scatter | solution.py:40
  (15 shorter events, 0.3 us)
Async XLA Ops:
  9.6 106.5 %all-to-all-start = ((f32[32,6,2048]{2,1,0:T(8,128)}), f32[32,6,2048]{2,1,0:T(8,128)S(1)}, u32[]{:S(2)}, u32[]{:S(2)}) async-start(f32[32,6,2048]{2,1,0:T(8,128)} %stack.12), calls=%async_computation | async-start | bytes 4194304 | tf_op jit(solution)/shard_map/all_to_all | solution.py:31
  117.6 102.2 %all-to-all-start.2 = ((f32[32,6,2048]{2,1,0:T(8,128)}), f32[32,6,2048]{2,1,0:T(8,128)}, u32[]{:S(2)}, u32[]{:S(2)}) async-start(f32[32,6,2048]{2,1,0:T(8,128)} %stack.13), calls=%async_computation.2 | async-start | bytes 4194304 | tf_op jit(solution)/shard_map/all_to_all | solution.py:31
  221.4 101.7 %all-to-all-start.4 = ((f32[32,6,2048]{2,1,0:T(8,128)}), f32[32,6,2048]{2,1,0:T(8,128)}, u32[]{:S(2)}, u32[]{:S(2)}) async-start(f32[32,6,2048]{2,1,0:T(8,128)} %stack.14), calls=%async_computation.4 | async-start | bytes 4194304 | tf_op jit(solution)/shard_map/all_to_all | solution.py:31
  324.6 101.8 %all-to-all-start.6 = ((f32[32,6,2048]{2,1,0:T(8,128)}), f32[32,6,2048]{2,1,0:T(8,128)}, u32[]{:S(2)}, u32[]{:S(2)}) async-start(f32[32,6,2048]{2,1,0:T(8,128)} %stack.15), calls=%async_computation.6 | async-start | bytes 4194304 | tf_op jit(solution)/shard_map/all_to_all | solution.py:31
  426.4 45.2 %all-to-all-start.1 = ((f32[192,16,128]{2,0,1:T(8,128)}), f32[192,16,128]{2,0,1:T(8,128)S(1)}, u32[]{:S(2)}, u32[]{:S(2)}) async-start(f32[192,16,128]{2,0,1:T(8,128)} %copy.24), calls=%async_computation.1 | async-start | bytes 3145728 | tf_op jit(solution)/shard_map/all_to_all | solution.py:33
  471.6 62.2 %all-to-all-start.3 = ((f32[192,16,128]{2,0,1:T(8,128)}), f32[192,16,128]{2,0,1:T(8,128)S(1)}, u32[]{:S(2)}, u32[]{:S(2)}) async-start(f32[192,16,128]{2,0,1:T(8,128)} %copy.28), calls=%async_computation.3 | async-start | bytes 3145728 | tf_op jit(solution)/shard_map/all_to_all | solution.py:33
  533.8 1.2 copy-start
  535.0 75.9 %all-to-all-start.5 = ((f32[192,16,128]{2,0,1:T(8,128)}), f32[192,16,128]{2,0,1:T(8,128)}, u32[]{:S(2)}, u32[]{:S(2)}) async-start(f32[192,16,128]{2,0,1:T(8,128)} %copy.32), calls=%async_computation.5 | async-start | bytes 3145728 | tf_op jit(solution)/shard_map/all_to_all | solution.py:33
  552.5 63.9 %copy-start.4 = (f32[256,4,128]{2,1,0:T(4,128)S(1)}, f32[256,4,128]{2,1,0:T(4,128)}, u32[]{:S(2)}) copy-start(f32[256,4,128]{2,1,0:T(4,128)} %param.3) | copy-start | bytes 1572868
  610.9 67.5 %all-to-all-start.7 = ((f32[192,16,128]{2,0,1:T(8,128)}), f32[192,16,128]{2,0,1:T(8,128)}, u32[]{:S(2)}, u32[]{:S(2)}) async-start(f32[192,16,128]{2,0,1:T(8,128)} %copy.36), calls=%async_computation.7 | async-start | bytes 3145728 | tf_op jit(solution)/shard_map/all_to_all | solution.py:33
  616.2 302.2 %reduce-scatter.2.cloned.1.call-start = ((), (), s32[]{:S(2)}) async-start(), calls=%async_computation.9 | async-start | bytes 3342336 | tf_op jit(solution)/shard_map/reduce_scatter | solution.py:40
  682.6 4.2 copy-start.1
  686.8 3.0 copy-start.2
  689.8 2.7 copy-start.3
Sparse Core Ops, SparseCore 0:
  697.0 221.3 reduce-scatter.1
